TPU v7x, 256 devices: a whole 4x4x8 slice. The times are simulated.
256 devices in a mesh: pipe: 8 (over x_lo, y), expert: 32 (over z, x_hi, core).
Axes of the slice: x: 4 (x_hi: 2, x_lo: 2; x = x_hi * 2 + x_lo), y: 4, z: 8, core: 2. Of those that a mesh axis runs over, the one named last changes fastest.
Arguments:
- tokens: bfloat16 [8, 4096, 2048], P('pipe', 'expert'), may hold values from -6 to 6
- routes: int32 [8, 4096, 6], P('pipe', 'expert'), may hold values from 0 to 31, all different within a row; in each aligned block of 128 rows (0 to 127, 128 to 255, ..., all dimensions but the last counted through in order) at most 36 rows name the same one
- norm_gain: float32 [8, 2048], P('pipe'), may hold values from 0.1 to 1.9
- router_weight: bfloat16 [8, 2048, 32], P('pipe'), may hold values from -0.125 to 0.125
- w_gate: bfloat16 [8, 32, 2048, 768], P('pipe', 'expert'), may hold values from -0.125 to 0.125
- w_up: bfloat16 [8, 32, 2048, 768], P('pipe', 'expert'), may hold values from -0.125 to 0.125
- w_down: bfloat16 [8, 32, 768, 2048], P('pipe', 'expert'), may hold values from -0.21875 to 0.21875
Outputs:
- received: bfloat16 [8, 4096, 2048], P('pipe', 'expert')
Inputs may be any that keep to these rules, and one draw needn't show every extreme that they name: Within each aligned block of 128 tokens of a section (the tokens of one device), the 6 routes of a token name different experts and no expert is named by more than 36 routes; some expert is named by exactly 36 routes in some block; every expert is named somewhere.
All inputs are finite; a program needn't handle non-finite values.
Results may differ from a plain program's by a relative error of at most 0.0039.
Values may be sent and summed in bfloat16 or wider, within the bound.
A program may use at most 128 MiB of HBM per device.

v0:
```python
import jax
import jax.numpy as jnp
from jax import lax
from jax.sharding import PartitionSpec as P


def shifted(shard, axis, by):
    devices = lax.axis_size(axis)
    return lax.ppermute(shard, axis, [(i, (i + by) % devices) for i in range(devices)])


def earlier_matrix(count):
    positions = jnp.arange(count, dtype=jnp.int32)
    return (positions[None, :] < positions[:, None]).astype(jnp.bfloat16)


def slot_ranks(route_block, experts):
    flat_routes = route_block.reshape(-1)
    hits = (flat_routes[:, None] == jnp.arange(experts, dtype=jnp.int32)[None, :]).astype(
        jnp.bfloat16
    )
    before = jnp.dot(earlier_matrix(flat_routes.shape[0]), hits, preferred_element_type=jnp.float32)
    ranks = jnp.sum(before * hits.astype(jnp.float32), axis=1).astype(jnp.int32)
    return ranks.reshape(route_block.shape)


def expert_ffn(slot_block, gate_matrix, up_matrix, down_matrix):
    gate_part = jnp.dot(slot_block, gate_matrix, preferred_element_type=jnp.float32)
    up_part = jnp.dot(slot_block, up_matrix, preferred_element_type=jnp.float32)
    hidden = (jax.nn.silu(gate_part) * up_part).astype(jnp.bfloat16)
    return jnp.dot(hidden, down_matrix, preferred_element_type=jnp.float32).astype(jnp.bfloat16)


def local(tokens, routes, norm_gain, router_weight, w_gate, w_up, w_down):
    local_rows = tokens[0]
    route_local = routes[0]
    gate_matrix = w_gate[0, 0]
    up_matrix = w_up[0, 0]
    down_matrix = w_down[0, 0]
    experts = lax.axis_size("expert")
    tok_dev, top_count = route_local.shape
    model_width = local_rows.shape[1]
    capacity = 3 * tok_dev * top_count // (2 * experts)
    wide_rows = local_rows.astype(jnp.float32)
    mean_square = jnp.mean(wide_rows * wide_rows, axis=-1, keepdims=True)
    normed = (wide_rows * lax.rsqrt(mean_square + 1e-06) * norm_gain[0]).astype(jnp.bfloat16)
    score = jax.nn.sigmoid(jnp.dot(normed, router_weight[0], preferred_element_type=jnp.float32))
    expert_ids = jnp.arange(experts, dtype=jnp.int32)
    chosen = route_local[..., None] == expert_ids[None, None, :]
    picked = jnp.sum(jnp.where(chosen, score[:, None, :], 0.0), axis=-1)
    gate_values = (picked / jnp.sum(picked, axis=1, keepdims=True)).astype(jnp.bfloat16)
    ranks = slot_ranks(route_local, experts)
    slots = route_local * capacity + ranks
    slot_hits = slots[..., None] == jnp.arange(experts * capacity, dtype=jnp.int32)[None, None, :]
    weights_map = jnp.sum(
        jnp.where(slot_hits, gate_values.astype(jnp.float32)[..., None], 0.0), axis=1
    ).astype(jnp.bfloat16)
    table = lax.all_gather(route_local, "expert", axis=0, tiled=True)
    gathered = lax.all_gather(normed, "expert", axis=0, tiled=True)
    own_index = lax.axis_index("expert")
    flat_count = tok_dev * top_count
    blocks = table.reshape(experts, flat_count)
    mine = blocks == own_index
    mine_values = mine.astype(jnp.bfloat16)
    own_ranks = jnp.dot(
        mine_values, earlier_matrix(flat_count).T, preferred_element_type=jnp.float32
    ).astype(jnp.int32)
    matches = mine[..., None] & (
        own_ranks[..., None] == jnp.arange(capacity, dtype=jnp.int32)[None, None, :]
    )
    selector = jnp.any(matches.reshape(experts, tok_dev, top_count, capacity), axis=2).astype(
        jnp.bfloat16
    )
    buffer = jnp.einsum(
        "btc,btd->bcd",
        selector,
        gathered.reshape(experts, tok_dev, model_width),
        preferred_element_type=jnp.float32,
    ).astype(jnp.bfloat16)
    owner_out = expert_ffn(buffer.reshape(-1, model_width), gate_matrix, up_matrix, down_matrix)
    returned = lax.all_to_all(
        owner_out.reshape(experts, capacity, model_width),
        "expert",
        split_axis=0,
        concat_axis=0,
        tiled=True,
    )
    moe = jnp.dot(
        weights_map,
        returned.reshape(experts * capacity, model_width),
        preferred_element_type=jnp.float32,
    )
    layer_out = (wide_rows + moe).astype(jnp.bfloat16)[None]
    received = shifted(layer_out, "pipe", 1)
    return received


def solution(mesh):
    return jax.shard_map(
        local,
        mesh=mesh,
        in_specs=(
            P("pipe", "expert", None),
            P("pipe", "expert", None),
            P("pipe", None),
            P("pipe", None, None),
            P("pipe", "expert", None, None),
            P("pipe", "expert", None, None),
            P("pipe", "expert", None, None),
        ),
        out_specs=P("pipe", "expert", None),
        check_vma=False,
    )
```

profile of v0, /device:TPU:2, one launch (start us, length us, event | category | flops | bytes accessed | tf_op | source)
XLA Modules:
  0.0 350.7 jit_solution(5233156969499989968)
XLA Ops:
  6.5 0.0 copy-start
  6.5 0.0 all-gather.3.cloned.1.call-start
  6.5 1.4 fusion.19
  7.9 2.0 fusion.21
  10.0 0.0 all-gather.3.cloned.1.call-update
  10.0 44.4 %all-gather = s32[1,4096,6]{1,0,2:T(1,128)S(1)} all-gather(s32[1,128,6]{1,0,2:T(1,128)} %param.8), channel_id=2, replica_groups=mesh['pipe'=8,'expert'=32] {'expert'}, dimensions={1}, use_global_device_ids=true | all-gather | bytes 101376 | tf_op jit(solution)/shard_map/all_gather | solution.py:58
  54.4 0.9 fusion.35
  55.3 1.5 copy.23
  56.8 2.5 eq.86
  59.3 1.0 fusion.14
  60.3 1.1 copy.24
  61.4 0.8 eq.87
  62.2 1.2 copy.25
  63.4 0.8 copy.33
  64.2 0.5 fusion.1
  64.7 85.4 %all-gather.3.cloned.1.call-done = bf16[4096,2048]{1,0:T(8,128)(2,1)} async-done(((bf16[128,2048]{1,0:T(8,128)(2,1)}), bf16[4096,2048]{1,0:T(8,128)(2,1)}) %all-gather.3.cloned.1.call-update) | async-done | bytes 16777232 | tf_op jit(solution)/shard_map/all_gather | solution.py:59
  150.0 10.4 %convolution_convert_fusion.1 = bf16[32,36,2048]{2,1,0:T(8,128)(2,1)} fusion(bf16[32,128,2048]{2,1,0:T(8,128)(2,1)} %bitcast.55, pred[32,128,36]{1,0,2:T(8,128)(4,1)S(1)} %fusion.1), kind=kOutput, calls=%fused_computation.1 | convolution fusion | flops 606339072 | bytes 21643264 | tf_op jit(solution)/shard_map/btc,btd->bcd/dot_general | solution.py:74
  160.4 7.2 %reshape.90 = bf16[1152,2048]{1,0:T(8,128)(2,1)} reshape(bf16[32,36,2048]{2,1,0:T(8,128)(2,1)} %convolution_convert_fusion.1) | data formatting | bytes 9437184 | tf_op jit(solution)/shard_map/reshape | solution.py:80
  167.7 0.0 copy-start.1
  167.7 0.0 copy-start.4
  167.7 6.8 %fusion.5 = f32[1152,768]{1,0:T(8,128)S(1)} fusion(bf16[1152,2048]{1,0:T(8,128)(2,1)} %reshape.90, bf16[1,1,2048,768]{3,2,1,0:T(8,128)(2,1)} %param.11), kind=kOutput, calls=%fused_computation.11 | convolution fusion | flops 3623878656 | bytes 11403264 | tf_op jit(solution)/shard_map/dot_general | solution.py:28
  174.4 0.0 copy-done.1
  174.4 0.0 copy-done.4
  174.4 4.2 %fusion.2 = bf16[1152,768]{1,0:T(8,128)(2,1)S(1)} fusion(bf16[1152,2048]{1,0:T(8,128)(2,1)S(1)} %copy-done.1, f32[1152,768]{1,0:T(8,128)S(1)} %fusion.5, bf16[1,1,2048,768]{3,2,1,0:T(8,128)(2,1)S(1)} %copy-done.4), kind=kOutput, calls=%fused_computation.8 | convolution fusion | flops 3629187072 | bytes 13172736 | tf_op jit(solution)/shard_map/dot_general | solution.py:29
  178.6 0.0 copy-done
  178.6 5.5 %convolution_convert_fusion = bf16[1152,2048]{1,0:T(8,128)(2,1)} fusion(bf16[1152,768]{1,0:T(8,128)(2,1)S(1)} %fusion.2, bf16[1,1,768,2048]{3,2,1,0:T(8,128)(2,1)S(1)} %copy-done), kind=kOutput, calls=%fused_computation | convolution fusion | flops 3626237952 | bytes 9633792 | tf_op jit(solution)/shard_map/dot_general | solution.py:31
  184.2 7.2 %reshape.91 = bf16[32,36,2048]{2,1,0:T(8,128)(2,1)} reshape(bf16[1152,2048]{1,0:T(8,128)(2,1)} %convolution_convert_fusion) | data formatting | bytes 9437184 | tf_op jit(solution)/shard_map/reshape | solution.py:82
  191.4 0.0 copy-start.2
  191.4 0.0 copy-start.3
  191.4 5.8 %all-to-all-start = ((bf16[32,36,2048]{2,1,0:T(8,128)(2,1)}), bf16[32,36,2048]{2,1,0:T(8,128)(2,1)}, u32[]{:S(2)}, u32[]{:S(2)}) async-start(bf16[32,36,2048]{2,1,0:T(8,128)(2,1)} %reshape.91), calls=%async_computation | async-start | bytes 10485760 | tf_op jit(solution)/shard_map/all_to_all | solution.py:81
  197.2 0.0 copy-done.2
  197.2 0.1 copy.19
  197.3 0.1 eq.73
  197.5 0.4 fusion.15
  197.8 0.1 convert_element_type.75
  198.0 0.1 copy.21
  198.1 0.0 copy-done.3
  198.1 1.5 fusion.18
  199.6 0.5 select_reduce_fusion
  200.1 116.3 %all-to-all-done = bf16[32,36,2048]{2,1,0:T(8,128)(2,1)} async-done(((bf16[32,36,2048]{2,1,0:T(8,128)(2,1)}), bf16[32,36,2048]{2,1,0:T(8,128)(2,1)}, u32[]{:S(2)}, u32[]{:S(2)}) %all-to-all-start) | async-done | bytes 4718624 | tf_op jit(solution)/shard_map/all_to_all | solution.py:81
  316.4 7.2 %reshape.92 = bf16[1152,2048]{1,0:T(8,128)(2,1)} reshape(bf16[32,36,2048]{2,1,0:T(8,128)(2,1)} %all-to-all-done) | data formatting | bytes 9437184 | tf_op jit(solution)/shard_map/reshape | solution.py:90
  323.6 3.3 fusion.10
  326.9 1.6 collective-permute-start
  328.5 14.5 %collective-permute-done = bf16[1,128,2048]{2,1,0:T(8,128)(2,1)S(1)} collective-permute-done((bf16[1,128,2048]{2,1,0:T(8,128)(2,1)S(1)}, bf16[1,128,2048]{2,1,0:T(8,128)(2,1)S(1)}, u32[]{:S(2)}, u32[]{:S(2)}) %collective-permute-start) | collective-permute-done | bytes 524320 | tf_op jit(solution)/shard_map/ppermute | solution.py:9
  343.0 0.8 copy.37
  (6 shorter events, 0.1 us)
Async XLA Ops:
  6.5 172.1 %copy-start = (bf16[1,1,768,2048]{3,2,1,0:T(8,128)(2,1)S(1)}, bf16[1,1,768,2048]{3,2,1,0:T(8,128)(2,1)}, u32[]{:S(2)}) copy-start(bf16[1,1,768,2048]{3,2,1,0:T(8,128)(2,1)} %param.13) | copy-start | bytes 9437188
  6.5 143.5 %all-gather.3.cloned.1.call-start = ((), (), s32[]{:S(2)}) async-start(), calls=%async_computation.1 | async-start | bytes 17301504 | tf_op jit(solution)/shard_map/all_gather | solution.py:59
  167.7 6.8 %copy-start.1 = (bf16[1152,2048]{1,0:T(8,128)(2,1)S(1)}, bf16[1152,2048]{1,0:T(8,128)(2,1)}, u32[]{:S(2)}) copy-start(bf16[1152,2048]{1,0:T(8,128)(2,1)} %reshape.90) | copy-start | bytes 14155780
  167.7 6.8 %copy-start.4 = (bf16[1,1,2048,768]{3,2,1,0:T(8,128)(2,1)S(1)}, bf16[1,1,2048,768]{3,2,1,0:T(8,128)(2,1)}, u32[]{:S(2)}) copy-start(bf16[1,1,2048,768]{3,2,1,0:T(8,128)(2,1)} %param.12) | copy-start | bytes 9437188
  191.4 5.8 %copy-start.2 = (s32[1,128,6]{1,0,2:T(1,128)S(1)}, s32[1,128,6]{1,0,2:T(1,128)}, u32[]{:S(2)}) copy-start(s32[1,128,6]{1,0,2:T(1,128)} %param.8) | copy-start | bytes 9220
  191.4 6.7 %copy-start.3 = (f32[1,2048]{1,0:T(1,128)S(1)}, f32[1,2048]{1,0:T(1,128)}, u32[]{:S(2)}) copy-start(f32[1,2048]{1,0:T(1,128)} %param.9) | copy-start | bytes 24580
  191.4 125.0 %all-to-all-start = ((bf16[32,36,2048]{2,1,0:T(8,128)(2,1)}), bf16[32,36,2048]{2,1,0:T(8,128)(2,1)}, u32[]{:S(2)}, u32[]{:S(2)}) async-start(bf16[32,36,2048]{2,1,0:T(8,128)(2,1)} %reshape.91), calls=%async_computation | async-start | bytes 10485760 | tf_op jit(solution)/shard_map/all_to_all | solution.py:81
  326.9 16.1 %collective-permute-start = (bf16[1,128,2048]{2,1,0:T(8,128)(2,1)S(1)}, bf16[1,128,2048]{2,1,0:T(8,128)(2,1)S(1)}, u32[]{:S(2)}, u32[]{:S(2)}) collective-permute-start(bf16[1,128,2048]{2,1,0:T(8,128)(2,1)S(1)} %fusion.10), channel_id=1, source_target_pairs={{0,32},{32,64},{64,96},{96,128},{128,160},{160,192},{192,224},{224... | collective-permute-start | bytes 1572872 | tf_op jit(solution)/shard_map/ppermute | solution.py:9
Sparse Core Ops, SparseCore 0:
  10.1 139.8 all-gather.2
where the time goes:
time: 352 us; the launch traced here: 351 us
  waiting for transfers between devices  216 us (61%)
  blocking collectives  44.4 us (13%)
  matrix products  32.9 us (9%)
  local copies, waits for them, and re-layouts  30.8 us (9%)
  between operations  13.5 us (4%)
  starting transfers between devices  7.39 us (2%)
  other arithmetic  5.4 us (2%)
    all_to_all x1, waiting for transfers between devices, local(): lax.all_to_all(owner_out.reshape(experts, capacity, model_width), 'expert...  116 us
    all_gather x1, waiting for transfers between devices, local(): gathered = lax.all_gather(normed, 'expert', axis=0, tiled=True)  85.4 us
    all_gather x1, blocking collectives, local(): table = lax.all_gather(route_local, 'expert', axis=0, tiled=True)  44.4 us
    ppermute x1, waiting for transfers between devices, shifted(): lax.ppermute(shard, axis, [(i, (i + by) % devices) for i in range(devices)])  14.5 us
    dot_general x1, matrix products, local(): jnp.einsum('btc,btd->bcd', selector, gathered.reshape(experts, tok_dev, m...  10.4 us
    reshape x1, local copies, waits for them, and re-layouts, local(): buffer.reshape(-1, model_width)  7.24 us
    reshape x1, local copies, waits for them, and re-layouts, local(): returned.reshape(experts * capacity, model_width)  7.22 us
    reshape x1, local copies, waits for them, and re-layouts, local(): owner_out.reshape(experts, capacity, model_width)  7.21 us
  transfers between devices with their start and end apart: 3, of which 3 were waited for; matrix products, arithmetic and copies ran while one was open for 4% of the time, Pallas kernels for 0%

commit v1 on v0

--- a/solution.py
+++ b/solution.py
@@ -56,7 +56,16 @@
         jnp.where(slot_hits, gate_values.astype(jnp.float32)[..., None], 0.0), axis=1
     ).astype(jnp.bfloat16)
     table = lax.all_gather(route_local, "expert", axis=0, tiled=True)
-    gathered = lax.all_gather(normed, "expert", axis=0, tiled=True)
+    rest_the_slots = lambda frame, axis_tag: jnp.concatenate(
+        lax.all_to_all(
+            jnp.stack([frame for _ in range(lax.axis_size(axis_tag))], 0),
+            axis_name=axis_tag,
+            split_axis=0,
+            concat_axis=0,
+        ),
+        0,
+    )
+    gathered = rest_the_slots(normed, "expert")
     own_index = lax.axis_index("expert")
     flat_count = tok_dev * top_count
     blocks = table.reshape(experts, flat_count)

time: 352 us -> 623 us (1.77)
  blocking collectives: 44.4 us -> 394 us
  waiting for transfers between devices: 216 us -> 131 us
  between operations: 13.5 us -> 0.19 us
  starting transfers between devices: 7.39 us -> 20.3 us
  local copies, waits for them, and re-layouts: 30.8 us -> 37.3 us
    all_gather x1, blocking collectives: 44.4 us -> 394 us  [local(): table = lax.all_gather(route_local, 'expert', axis=0, tiled=True)]
    all_gather x1 -> x0, waiting for transfers between devices: 85.4 us -> none  [local(): gathered = lax.all_gather(normed, 'expert', axis=0, tiled=True)]
    all_to_all x0 -> x1, starting transfers between devices: none -> 10.7 us  [local(): lax.all_to_all(jnp.stack([frame for _ in range(lax.axis_size(axis_tag))],...]
  transfers between devices with their start and end apart: 3 -> 3, of which waited for: 3 -> 2; matrix products, arithmetic and copies ran while one was open for 4% -> 2% of each run, Pallas kernels for 0% -> 0%
where the time goes in v1:
time: 623 us; the launch traced here: 620 us
  blocking collectives  394 us (63%)
  waiting for transfers between devices  131 us (21%)
  local copies, waits for them, and re-layouts  37.3 us (6%)
  matrix products  32.9 us (5%)
  starting transfers between devices  20.3 us (3%)
    all_gather x1, blocking collectives, local(): table = lax.all_gather(route_local, 'expert', axis=0, tiled=True)  394 us
    all_to_all x1, waiting for transfers between devices, local(): lax.all_to_all(owner_out.reshape(experts, capacity, model_width), 'expert...  116 us
    ppermute x1, waiting for transfers between devices, shifted(): lax.ppermute(shard, axis, [(i, (i + by) % devices) for i in range(devices)])  14.5 us
  transfers between devices with their start and end apart: 3, of which 2 were waited for; matrix products, arithmetic and copies ran while one was open for 2% of the time, Pallas kernels for 0%

profile of v1, /device:TPU:2, one launch (start us, length us, event | category | flops | bytes accessed | tf_op | source)
XLA Modules:
  0.0 620.5 jit_solution(9066624061285226528)
XLA Ops:
  0.0 0.0 copy-start
  0.0 1.4 fusion.18
  1.4 1.2 fusion.22
  2.6 0.0 copy-start.1
  2.6 0.8 copy-done.1
  3.4 5.9 stack.2
  9.4 0.0 copy-start.4
  9.4 10.7 %all-to-all-start = ((bf16[32,128,2048]{2,1,0:T(8,128)(2,1)}), bf16[32,128,2048]{2,1,0:T(8,128)(2,1)}, u32[]{:S(2)}, u32[]{:S(2)}) async-start(bf16[32,128,2048]{2,1,0:T(8,128)(2,1)} %stack.2), calls=%async_computation | async-start | bytes 33554432 | tf_op jit(solution)/shard_map/all_to_all | solution.py:60
  20.1 0.0 copy-done.4
  20.1 394.1 %all-gather = s32[1,4096,6]{1,0,2:T(1,128)S(1)} all-gather(s32[1,128,6]{1,0,2:T(1,128)S(1)} %copy-done.4), channel_id=2, replica_groups=mesh['pipe'=8,'expert'=32] {'expert'}, dimensions={1}, use_global_device_ids=true | all-gather | bytes 101376 | tf_op jit(solution)/shard_map/all_gather | solution.py:58
  414.2 0.3 fusion.29
  414.5 0.6 copy.33
  415.1 1.5 copy.23
  416.6 2.5 eq.86
  419.1 1.0 fusion.13
  420.1 1.1 copy.24
  421.2 0.8 eq.87
  422.0 1.2 copy.25
  423.2 1.2 fusion.1
  424.5 0.0 all-to-all-done
  424.5 10.4 %convolution_convert_fusion.1 = bf16[32,36,2048]{2,1,0:T(8,128)(2,1)} fusion(bf16[32,128,2048]{2,1,0:T(8,128)(2,1)} %all-to-all-done, pred[32,128,36]{1,0,2:T(8,128)(4,1)S(1)} %fusion.1), kind=kOutput, calls=%fused_computation.1 | convolution fusion | flops 606339072 | bytes 21643264 | tf_op jit(solution)/shard_map/btc,btd->bcd/dot_general | solution.py:83
  434.9 7.2 %reshape.100 = bf16[1152,2048]{1,0:T(8,128)(2,1)} reshape(bf16[32,36,2048]{2,1,0:T(8,128)(2,1)} %convolution_convert_fusion.1) | data formatting | bytes 9437184 | tf_op jit(solution)/shard_map/reshape | solution.py:89
  442.1 0.0 copy-start.2
  442.1 0.0 copy-start.5
  442.1 6.8 %fusion.5 = f32[1152,768]{1,0:T(8,128)S(1)} fusion(bf16[1152,2048]{1,0:T(8,128)(2,1)} %reshape.100, bf16[1,1,2048,768]{3,2,1,0:T(8,128)(2,1)} %param.11), kind=kOutput, calls=%fused_computation.11 | convolution fusion | flops 3623878656 | bytes 11403264 | tf_op jit(solution)/shard_map/dot_general | solution.py:28
  448.9 0.0 copy-done.2
  448.9 0.0 copy-done.5
  448.9 4.2 fusion.2
  453.1 0.0 copy-done
  453.1 5.5 convolution_convert_fusion
  458.6 7.2 %reshape.101 = bf16[32,36,2048]{2,1,0:T(8,128)(2,1)} reshape(bf16[1152,2048]{1,0:T(8,128)(2,1)} %convolution_convert_fusion) | data formatting | bytes 9437184 | tf_op jit(solution)/shard_map/reshape | solution.py:91
  465.8 0.0 copy-start.3
  465.8 8.0 %all-to-all-start.1 = ((bf16[32,36,2048]{2,1,0:T(8,128)(2,1)}), bf16[32,36,2048]{2,1,0:T(8,128)(2,1)}, u32[]{:S(2)}, u32[]{:S(2)}) async-start(bf16[32,36,2048]{2,1,0:T(8,128)(2,1)} %reshape.101), calls=%async_computation.1 | async-start | bytes 10485760 | tf_op jit(solution)/shard_map/all_to_all | solution.py:90
  473.8 0.1 copy.19
  473.9 0.1 eq.73
  474.1 0.4 fusion.14
  474.4 0.1 convert_element_type.75
  474.6 0.1 copy.21
  474.6 0.0 copy-done.3
  474.6 1.4 fusion.17
  476.1 0.5 select_reduce_fusion
  476.6 116.4 %all-to-all-done.1 = bf16[32,36,2048]{2,1,0:T(8,128)(2,1)} async-done(((bf16[32,36,2048]{2,1,0:T(8,128)(2,1)}), bf16[32,36,2048]{2,1,0:T(8,128)(2,1)}, u32[]{:S(2)}, u32[]{:S(2)}) %all-to-all-start.1) | async-done | bytes 4718624 | tf_op jit(solution)/shard_map/all_to_all | solution.py:90
  593.0 7.2 %reshape.102 = bf16[1152,2048]{1,0:T(8,128)(2,1)} reshape(bf16[32,36,2048]{2,1,0:T(8,128)(2,1)} %all-to-all-done.1) | data formatting | bytes 9437184 | tf_op jit(solution)/shard_map/reshape | solution.py:99
  600.2 3.3 fusion.10
  603.5 1.7 collective-permute-start
  605.2 14.5 %collective-permute-done = bf16[1,128,2048]{2,1,0:T(8,128)(2,1)S(1)} collective-permute-done((bf16[1,128,2048]{2,1,0:T(8,128)(2,1)S(1)}, bf16[1,128,2048]{2,1,0:T(8,128)(2,1)S(1)}, u32[]{:S(2)}, u32[]{:S(2)}) %collective-permute-start) | collective-permute-done | bytes 524320 | tf_op jit(solution)/shard_map/ppermute | solution.py:9
  619.7 0.8 copy.37
  (6 shorter events, 0.1 us)
Async XLA Ops:
  0.0 453.1 %copy-start = (bf16[1,1,768,2048]{3,2,1,0:T(8,128)(2,1)S(1)}, bf16[1,1,768,2048]{3,2,1,0:T(8,128)(2,1)}, u32[]{:S(2)}) copy-start(bf16[1,1,768,2048]{3,2,1,0:T(8,128)(2,1)} %param.13) | copy-start | bytes 9437188
  2.6 0.8 copy-start.1
  9.4 10.7 %copy-start.4 = (s32[1,128,6]{1,0,2:T(1,128)S(1)}, s32[1,128,6]{1,0,2:T(1,128)}, u32[]{:S(2)}) copy-start(s32[1,128,6]{1,0,2:T(1,128)} %param.8) | copy-start | bytes 9220
  9.4 415.1 %all-to-all-start = ((bf16[32,128,2048]{2,1,0:T(8,128)(2,1)}), bf16[32,128,2048]{2,1,0:T(8,128)(2,1)}, u32[]{:S(2)}, u32[]{:S(2)}) async-start(bf16[32,128,2048]{2,1,0:T(8,128)(2,1)} %stack.2), calls=%async_computation | async-start | bytes 33554432 | tf_op jit(solution)/shard_map/all_to_all | solution.py:60
  442.1 6.8 %copy-start.2 = (bf16[1152,2048]{1,0:T(8,128)(2,1)S(1)}, bf16[1152,2048]{1,0:T(8,128)(2,1)}, u32[]{:S(2)}) copy-start(bf16[1152,2048]{1,0:T(8,128)(2,1)} %reshape.100) | copy-start | bytes 14155780
  442.1 6.8 %copy-start.5 = (bf16[1,1,2048,768]{3,2,1,0:T(8,128)(2,1)S(1)}, bf16[1,1,2048,768]{3,2,1,0:T(8,128)(2,1)}, u32[]{:S(2)}) copy-start(bf16[1,1,2048,768]{3,2,1,0:T(8,128)(2,1)} %param.12) | copy-start | bytes 9437188
  465.8 8.8 %copy-start.3 = (bf16[1,2048,32]{1,2,0:T(8,128)(2,1)S(1)}, bf16[1,2048,32]{1,2,0:T(8,128)(2,1)}, u32[]{:S(2)}) copy-start(bf16[1,2048,32]{1,2,0:T(8,128)(2,1)} %param.10) | copy-start | bytes 393220
  465.8 127.2 %all-to-all-start.1 = ((bf16[32,36,2048]{2,1,0:T(8,128)(2,1)}), bf16[32,36,2048]{2,1,0:T(8,128)(2,1)}, u32[]{:S(2)}, u32[]{:S(2)}) async-start(bf16[32,36,2048]{2,1,0:T(8,128)(2,1)} %reshape.101), calls=%async_computation.1 | async-start | bytes 10485760 | tf_op jit(solution)/shard_map/all_to_all | solution.py:90
  603.5 16.1 %collective-permute-start = (bf16[1,128,2048]{2,1,0:T(8,128)(2,1)S(1)}, bf16[1,128,2048]{2,1,0:T(8,128)(2,1)S(1)}, u32[]{:S(2)}, u32[]{:S(2)}) collective-permute-start(bf16[1,128,2048]{2,1,0:T(8,128)(2,1)S(1)} %fusion.10), channel_id=1, source_target_pairs={{0,32},{32,64},{64,96},{96,128},{128,160},{160,192},{192,224},{224... | collective-permute-start | bytes 1572872 | tf_op jit(solution)/shard_map/ppermute | solution.py:9
